TPU v7x, 32 devices: a whole 2x2x4 slice. The times are simulated.
32 devices in a mesh: samp: 2 (over x), cpg: 16 (over z, y, core).
Axes of the slice: x: 2, y: 2, z: 4, core: 2. Of those that a mesh axis runs over, the one named last changes fastest.
Arguments:
- methylation: bfloat16 [512, 114688], P('samp', 'cpg'), may hold values from -6 to 6
- labels: int32 [512], P('samp'), may hold values from 0 to 31, as said below
- directions: bfloat16 [8, 114688], P(None, 'cpg'), may hold values from -0.015625 to 0.015625
- step_sizes: float32 [8], replicated, may hold values from 0.05 to 1.5
- supports: int32 [8, 64], replicated, may hold values from 0 to 895, as said below
Outputs:
- new_directions: float32 [8, 114688], P(None, 'cpg')
- quotients: float32 [8], replicated
Inputs may be any that keep to these rules, and one draw needn't show every extreme that they name: Every class from 0 to 31 labels at least one sample. `supports`: each row holds 64 different block indices.
All inputs are finite; a program needn't handle non-finite values.
Results may differ from a plain program's by a relative error of at most 0.0026.
Values sent between devices are 32-bit elements; how exact they have to be, the bound alone decides.
A program may use at most 64 MiB of HBM per device.

v0:
```python
import jax
import jax.numpy as jnp
from jax import lax
from jax.sharding import PartitionSpec as P

CLASSES = 32
BLOCK = 128
KB = 64


STABILITY_FLOOR = 1e-06


def block_mask(supports, first_block, count):
    block_ids = first_block + jnp.arange(count, dtype=jnp.int32)
    hits = jnp.any(supports[:, :, None] == block_ids[None, None, :], axis=1)
    return jnp.repeat(hits.astype(jnp.float32), BLOCK, axis=1)


def per_device(methylation, labels, directions, step_sizes, supports):
    highest = lax.Precision.HIGHEST
    local_cols = methylation.shape[1]
    onehot = (labels[:, None] == jnp.arange(CLASSES, dtype=jnp.int32)[None, :]).astype(jnp.float32)
    partial_proj = lax.dot_general(
        methylation, directions, (((1,), (1,)), ((), ())), preferred_element_type=jnp.float32
    )
    projected = lax.psum(partial_proj, "cpg")
    local_class = jnp.dot(onehot.T, projected, precision=highest)
    local_counts = jnp.sum(onehot, axis=0)
    class_proj, counts, total_sq = lax.psum(
        (local_class, local_counts, jnp.sum(projected * projected, axis=0)), "samp"
    )
    mean_proj = class_proj / counts[:, None]
    within = projected - jnp.dot(onehot, mean_proj, precision=highest)
    within_q = total_sq - jnp.sum(class_proj * mean_proj, axis=0)
    grand = jnp.sum(class_proj, axis=0) / jnp.sum(counts)
    between_q = jnp.sum((mean_proj - grand[None, :]) * class_proj, axis=0)
    quotients = between_q / within_q
    combined = (
        jnp.dot(onehot, mean_proj - grand[None, :], precision=highest) - quotients[None, :] * within
    ).astype(jnp.bfloat16)
    partial_grad = lax.dot_general(
        combined, methylation, (((0,), (0,)), ((), ())), preferred_element_type=jnp.float32
    )
    step_scale = (step_sizes / within_q)[:, None]
    first_block = lax.axis_index("cpg") * (local_cols // BLOCK)
    kept_mask = block_mask(supports, first_block, local_cols // BLOCK)
    gradient = lax.psum(partial_grad, "samp")
    updated = directions.astype(jnp.float32) + step_scale * gradient
    masked = updated * kept_mask
    sums = lax.psum(jnp.sum(masked * masked, axis=1), "cpg")
    new_directions = masked * lax.rsqrt(sums / (KB * BLOCK) + STABILITY_FLOOR)[:, None]
    return (new_directions, quotients)


def solution(mesh):
    in_specs = (P("samp", "cpg"), P("samp"), P(None, "cpg"), P(), P())
    out_specs = (P(None, "cpg"), P())
    return jax.shard_map(
        per_device, mesh=mesh, in_specs=in_specs, out_specs=out_specs, check_vma=False
    )
```

profile of v0, /device:TPU:0, one launch (start us, length us, event | category | flops | bytes accessed | tf_op | source)
XLA Modules:
  0.0 119.8 jit_solution(10647501636812897144)
XLA Ops:
  7.2 0.0 copy-start.2
  7.2 0.0 copy-start.3
  7.2 0.0 all-reduce.3.cloned.1.call-start
  7.2 0.8 convert_reduce_fusion
  8.0 0.0 copy-start.1
  8.0 0.0 copy-start
  8.1 3.1 %fusion.11 = f32[256,8]{0,1:T(8,128)S(1)} fusion(bf16[256,7168]{1,0:T(8,128)(2,1)} %param.5, bf16[8,7168]{1,0:T(8,128)(2,1)} %param.7), kind=kOutput, calls=%fused_computation.26 | convolution fusion | flops 29360128 | bytes 3792896 | tf_op jit(solution)/shard_map/dot_general | solution.py:24
  11.2 35.5 %psum.42 = f32[256,8]{0,1:T(8,128)S(1)} all-reduce(f32[256,8]{0,1:T(8,128)S(1)} %fusion.11), channel_id=1, replica_groups=mesh['samp'=2,'cpg'=16] {'cpg'}, use_global_device_ids=true, to_apply=%region_0.0 | all-reduce | flops 2048 | bytes 16384 | tf_op jit(solution)/shard_map/psum | solution.py:27
  46.6 0.1 multiply_reduce_fusion.1
  46.8 0.0 copy-done.2
  46.8 0.1 fusion.5
  46.9 5.0 %all-reduce = (f32[32,8]{0,1:T(8,128)S(1)}, f32[32]{0:T(128)S(1)}, f32[8]{0:T(128)S(1)}) all-reduce(f32[32,8]{0,1:T(8,128)S(1)} %fusion.5, f32[32]{0:T(128)S(1)} %convert_reduce_fusion, f32[8]{0:T(128)S(1)} %multiply_reduce_fusion.1), channel_id=1, replica_groups=mesh['samp'=2,'cpg'=16] {'samp'}, use_global_device_ids=true, to_apply=%region_3.0 | all-reduce | flops 296 | bytes 2368 | tf_op jit(solution)/shard_map/psum | solution.py:30
  51.9 0.6 reduce_sum.67
  52.5 0.1 reduce_sum.66
  52.6 0.7 broadcast_divide_fusion.1
  53.2 0.2 multiply_reduce_fusion.3
  53.4 0.2 fusion.4
  53.6 0.0 copy-done.3
  53.6 0.0 copy-start.4
  53.6 0.1 fusion.2
  53.7 3.4 %fusion.12 = f32[8,7168]{1,0:T(8,128)} fusion(bf16[256,8]{0,1:T(8,128)(2,1)S(1)} %fusion.2, bf16[256,7168]{1,0:T(8,128)(2,1)} %param.5), kind=kOutput, calls=%fused_computation.27 | convolution fusion | flops 29360128 | bytes 3903488 | tf_op jit(solution)/shard_map/dot_general | solution.py:42
  57.1 0.0 all-reduce.3.cloned.1.call-update
  57.1 0.0 copy-done.1
  57.2 0.3 compare_reduce_fusion
  57.4 0.1 copy.7
  57.5 19.9 %all-reduce.3.cloned.1.call-done = f32[8,7168]{1,0:T(8,128)} async-done(((f32[8,7168]{1,0:T(8,128)}), f32[8,7168]{1,0:T(8,128)}) %all-reduce.3.cloned.1.call-update) | async-done | bytes 229392 | tf_op jit(solution)/shard_map/psum | solution.py:48
  77.4 0.0 copy-done
  77.4 1.2 multiply_reduce_fusion
  78.6 32.7 %psum.47 = f32[8]{0:T(128)S(1)} all-reduce(f32[8]{0:T(128)S(1)} %multiply_reduce_fusion), channel_id=1, replica_groups=mesh['samp'=2,'cpg'=16] {'cpg'}, use_global_device_ids=true, to_apply=%region_13.0 | all-reduce | flops 8 | bytes 64 | tf_op jit(solution)/shard_map/psum | solution.py:51
  111.2 1.8 %fusion.3 = f32[8,7168]{1,0:T(8,128)} fusion(f32[8,7168]{1,0:T(8,128)} %all-reduce.3.cloned.1.call-done, bf16[8,7168]{1,0:T(8,128)(2,1)S(1)} %copy-done, f32[8]{0:T(128)S(1)} %add_rsqrt_fusion, f32[8,56]{0,1:T(8,128)S(1)} %copy.7, f32[8]{0:T(128)S(1)} %get-tuple-element.7), kind=kLoop, calls=%fused_computation.7 | loop fusion | flops 286720 | bytes 575296 | tf_op jit(solution)/shard_map/mul | solution.py:52
  113.0 0.0 copy-done.4
  (4 shorter events, 0.0 us)
Async XLA Ops:
  7.2 39.6 %copy-start.2 = (s32[256]{0:T(256)S(1)}, s32[256]{0:T(256)}, u32[]{:S(2)}) copy-start(s32[256]{0:T(256)} %param.6) | copy-start | bytes 3076
  7.2 46.4 %copy-start.3 = (f32[8]{0:T(128)S(1)}, f32[8]{0:T(128)}, u32[]{:S(2)}) copy-start(f32[8]{0:T(128)} %param.8) | copy-start | bytes 100
  7.2 70.2 %all-reduce.3.cloned.1.call-start = ((), (), s32[]{:S(2)}) async-start(), calls=%async_computation | async-start | bytes 458752 | tf_op jit(solution)/shard_map/psum | solution.py:48
  8.0 49.1 %copy-start.1 = (s32[8,64]{1,0:T(8,128)S(1)}, s32[8,64]{1,0:T(8,128)}, u32[]{:S(2)}) copy-start(s32[8,64]{1,0:T(8,128)} %param.9) | copy-start | bytes 6148
  8.0 69.4 %copy-start = (bf16[8,7168]{1,0:T(8,128)(2,1)S(1)}, bf16[8,7168]{1,0:T(8,128)(2,1)}, u32[]{:S(2)}) copy-start(bf16[8,7168]{1,0:T(8,128)(2,1)} %param.7) | copy-start | bytes 344068
  53.6 59.4 %copy-start.4 = (f32[8]{0:T(128)}, f32[8]{0:T(128)S(1)}, u32[]{:S(2)}) copy-start(f32[8]{0:T(128)S(1)} %get-tuple-element.8) | copy-start | bytes 100
Sparse Core Ops, SparseCore 0:
  57.2 20.0 all-reduce.2
where the time goes:
time: 120 us
  blocking collectives  73.1 us (61%)
  waiting for transfers between devices  19.9 us (17%)
  between operations  14.1 us (12%)
  matrix products  6.9 us (6%)
  other arithmetic  5.71 us (5%)
    psum x1, blocking collectives, per_device(): projected = lax.psum(partial_proj, 'cpg')  35.5 us
    psum x1, blocking collectives, per_device(): sums = lax.psum(jnp.sum(masked * masked, axis=1), 'cpg')  32.7 us
    psum x1, waiting for transfers between devices, per_device(): gradient = lax.psum(partial_grad, 'samp')  19.9 us
    psum x1, blocking collectives, per_device(): lax.psum((local_class, local_counts, jnp.sum(projected * projected, axis=...  4.96 us
    dot_general x1, matrix products, per_device(): lax.dot_general(combined, methylation, (((0,), (0,)), ((), ())), preferre...  3.37 us
    dot_general x1, matrix products, per_device(): lax.dot_general(methylation, directions, (((1,), (1,)), ((), ())), prefer...  3.12 us
  transfers between devices with their start and end apart: 1, of which 1 were waited for; matrix products, arithmetic and copies ran while one was open for 0% of the time, Pallas kernels for 0%

commit v1 on v0

v1 whole, which is shorter than its diff:
```python
import functools

import jax
import jax.numpy as jnp
from jax import lax
from jax.experimental import pallas as pl
from jax.experimental.pallas import tpu as pltpu
from jax.sharding import PartitionSpec as P

CLASSES = 32
BLOCK = 128
STABILITY_FLOOR = 1e-06
MESH = pl.DeviceIdType.MESH
F32 = jnp.float32
BF16 = jnp.bfloat16
NT = (((1,), (1,)), ((), ()))
NN = (((1,), (0,)), ((), ()))


def divisor(n, most):
    return max(d for d in range(1, most + 1) if n % d == 0)


def split3(x):
    high = x.astype(BF16).astype(F32)
    rest = x - high
    mid = rest.astype(BF16).astype(F32)
    return [high, mid, (rest - mid).astype(BF16).astype(F32)]


def eye_of(rows, lanes):
    return lax.broadcasted_iota(jnp.int32, (rows, lanes), 0) == lax.broadcasted_iota(
        jnp.int32, (rows, lanes), 1
    )


def to_row(col, lanes):
    rows = col.shape[0]
    return jnp.sum(jnp.where(eye_of(rows, lanes), col, 0.0), axis=0, keepdims=True)


def to_col(row, rows):
    return jnp.sum(jnp.where(eye_of(rows, row.shape[1]), row, 0.0), axis=1, keepdims=True)


def kernel(
    S, C, A, nk, nch,
    m_hbm, d_hbm, lab_ref, step_ref, sup_ref,
    out_ref, quo_ref,
    mv, dv, part, abuf, bbuf, pall, proj, lab_all, gsend, grecv, fbuf, sbuf, mask,
    m_sem, d_sem, lab_send, lab_recv, a_send, a_recv, b_send, b_recv, c_send, c_recv,
    g_send, g_recv, f_send, f_recv, s_send, s_recv,
):
    B = C // A
    N = S * C
    G = S * A
    rows, cols = mv.shape
    dirs = dv.shape[0]
    R = dirs // A
    ck = cols // nk
    piece = cols // S
    ch = piece // nch
    s = lax.axis_index("samp")
    c = lax.axis_index("cpg")
    a = lax.rem(c, A)
    b = lax.div(c, A)
    me = s * C + c
    mine = s * A + a

    d_copy = pltpu.make_async_copy(d_hbm, dv, d_sem)
    d_copy.start()
    m_copies = []
    for k in range(nk):
        span = pl.ds(k * ck, ck)
        copy = pltpu.make_async_copy(m_hbm.at[:, span], mv.at[:, span], m_sem.at[k])
        copy.start()
        m_copies.append(copy)

    barrier = pltpu.get_barrier_semaphore()

    def greet(r, carry):
        t = lax.rem(me + r, N)
        pl.semaphore_signal(
            barrier, inc=1, device_id=(lax.div(t, C), lax.rem(t, C)), device_id_type=MESH
        )
        return carry

    lax.fori_loop(1, N, greet, 0)

    lab_all[s] = lab_ref[...]
    sup = sup_ref[...]
    first = c * (cols // BLOCK) + s * (piece // BLOCK)
    for k in range(nch):
        for j in range(ch // BLOCK):
            hit = jnp.max(
                jnp.where(sup == first + (k * (ch // BLOCK) + j), 1.0, 0.0), axis=1, keepdims=True
            )
            mask[k, :, j * BLOCK:(j + 1) * BLOCK] = jnp.broadcast_to(hit, (dirs, BLOCK))

    d_copy.wait()
    acc = jnp.zeros((dirs, rows), F32)
    for k in range(nk):
        m_copies[k].wait()
        acc = acc + lax.dot_general(
            dv[:, k * ck:(k + 1) * ck], mv[:, k * ck:(k + 1) * ck], NT, preferred_element_type=F32
        )
    for i in range(A):
        part[i] = acc[i * R:(i + 1) * R, :]

    pl.semaphore_wait(barrier, N - 1)

    def remote(src, dst, send, recv, to):
        return pltpu.make_async_remote_copy(
            src_ref=src, dst_ref=dst, send_sem=send, recv_sem=recv, device_id=to,
            device_id_type=MESH,
        )

    sent = []

    def start(copy):
        copy.start()
        sent.append(copy)

    for r in range(1, A):
        t = lax.rem(a + r, A)
        start(remote(part.at[t], abuf.at[a], a_send.at[r], a_recv.at[a], (s, b * A + t)))
    for r in range(1, S):
        t = lax.rem(s + r, S)
        start(remote(lab_ref, lab_all.at[s], lab_send.at[r], lab_recv.at[s], (t, c)))
    abuf[a] = part[a]
    for r in range(1, A):
        t = lax.rem(a + r, A)
        remote(part.at[t], abuf.at[t], a_send.at[r], a_recv.at[t], (s, c)).wait_recv()
    bbuf[b] = functools.reduce(jnp.add, [abuf[i] for i in range(A)])
    for r in range(1, B):
        t = lax.rem(b + r, B)
        start(remote(bbuf.at[b], bbuf.at[b], b_send.at[r], b_recv.at[b], (s, t * A + a)))
    for r in range(1, B):
        t = lax.rem(b + r, B)
        remote(bbuf.at[t], bbuf.at[t], b_send.at[r], b_recv.at[t], (s, c)).wait_recv()
    pall[mine] = functools.reduce(jnp.add, [bbuf[i] for i in range(B)])
    for r in range(1, G):
        t = lax.rem(mine + r, G)
        to = (lax.div(t, A), b * A + lax.rem(t, A))
        start(remote(pall.at[mine], pall.at[mine], c_send.at[r], c_recv.at[mine], to))
    for r in range(1, S):
        t = lax.rem(s + r, S)
        remote(lab_ref, lab_all.at[t], lab_send.at[r], lab_recv.at[t], (s, c)).wait_recv()
    classes = lax.broadcasted_iota(jnp.int32, (CLASSES, rows), 0)
    onehot = [(classes == lab_all[i]).astype(F32).astype(BF16) for i in range(S)]
    for r in range(1, G):
        t = lax.rem(mine + r, G)
        remote(pall.at[t], pall.at[t], c_send.at[r], c_recv.at[t], (s, c)).wait_recv()

    stats = jnp.zeros((4 * dirs, CLASSES), F32)
    for i in range(S):
        for j in range(A):
            proj[i, j * R:(j + 1) * R, :] = pall[i * A + j]
        left = jnp.concatenate(split3(proj[i]) + [jnp.ones((dirs, rows), F32)], axis=0)
        stats = stats + lax.dot_general(left.astype(BF16), onehot[i], NT, preferred_element_type=F32)
    class_proj = stats[:dirs] + stats[dirs:2 * dirs] + stats[2 * dirs:3 * dirs]
    mean_proj = class_proj / stats[3 * dirs:]
    grand = jnp.sum(class_proj, axis=1, keepdims=True) / (S * rows)
    between_q = jnp.sum((mean_proj - grand) * class_proj, axis=1, keepdims=True)
    left = jnp.concatenate(split3(mean_proj), axis=0).astype(BF16)

    def expand(hot):
        e = lax.dot_general(left, hot, NN, preferred_element_type=F32)
        return e[:dirs] + e[dirs:2 * dirs] + e[2 * dirs:]

    squares = jnp.zeros((dirs, rows), F32)
    for i in range(S):
        within = proj[i] - expand(onehot[i])
        squares = squares + within * within
    within_q = jnp.sum(squares, axis=1, keepdims=True)
    quotients = between_q / within_q
    own = expand((classes == lab_ref[...]).astype(F32).astype(BF16))
    combined = ((own - grand) - quotients * (proj[s] - own)).astype(BF16)
    scale = to_col(step_ref[...], dirs) / within_q
    quo_ref[...] = to_row(quotients, dirs)

    for r in list(range(1, S)) + [0]:
        t = lax.rem(s + r, S)
        for k in range(nch):
            span = pl.ds(pl.multiple_of(t * piece + k * ch, BLOCK), ch)
            g = jnp.dot(combined, mv[:, span], preferred_element_type=F32)
            if r == 0:
                grecv[s, k] = g
            else:
                gsend[r - 1, k] = g
                start(remote(
                    gsend.at[r - 1, k], grecv.at[s, k], g_send.at[r, k], g_recv.at[s, k], (t, c)
                ))
    total = jnp.zeros((dirs, ch), F32)
    for k in range(nch):
        for r in range(1, S):
            t = lax.rem(s + r, S)
            remote(
                gsend.at[r - 1, k], grecv.at[t, k], g_send.at[r, k], g_recv.at[t, k], (s, c)
            ).wait_recv()
        g = functools.reduce(jnp.add, [grecv[i, k] for i in range(S)])
        span = pl.ds(pl.multiple_of(s * piece + k * ch, BLOCK), ch)
        kept = (dv[:, span].astype(F32) + scale * g) * mask[k]
        fbuf[s, k] = kept
        total = total + kept * kept
    sbuf[me] = to_row(jnp.sum(total, axis=1, keepdims=True), BLOCK)

    def tell(r, carry):
        t = lax.rem(me + r, N)
        remote(
            sbuf.at[me], sbuf.at[me], s_send, s_recv, (lax.div(t, C), lax.rem(t, C))
        ).start()
        return carry

    lax.fori_loop(1, N, tell, 0)
    for r in range(1, S):
        t = lax.rem(s + r, S)
        start(remote(fbuf.at[s], fbuf.at[s], f_send.at[r], f_recv.at[s], (t, c)))
    others = sbuf.at[pl.ds(0, N - 1)]
    pltpu.make_async_copy(others, others, s_recv).wait()
    sums = to_col(jnp.sum(sbuf[...], axis=0), dirs)
    norm = lax.rsqrt(sums / (sup_ref.shape[1] * BLOCK) + STABILITY_FLOOR)
    for r in range(1, S):
        t = lax.rem(s + r, S)
        remote(fbuf.at[t], fbuf.at[t], f_send.at[r], f_recv.at[t], (s, c)).wait_recv()
    for i in range(S):
        for k in range(nch):
            at = i * piece + k * ch
            out_ref[:, at:at + ch] = fbuf[i, k] * norm
    for copy in sent:
        copy.wait_send()
    pltpu.make_async_copy(others, others, s_send).wait()


def per_device(S, C, methylation, labels, directions, step_sizes, supports):
    rows, cols = methylation.shape
    dirs = directions.shape[0]
    A = max(d for d in range(1, dirs + 1) if dirs % d == 0 and C % d == 0 and d * d <= C)
    B, N, G, R = C // A, S * C, S * A, dirs // A
    piece = cols // S
    nk = divisor(cols // BLOCK, 7)
    nch = divisor(piece // BLOCK, 4)
    ch = piece // nch
    dma = pltpu.SemaphoreType.DMA
    vmem = pl.BlockSpec(memory_space=pltpu.VMEM)
    hbm = pl.BlockSpec(memory_space=pltpu.HBM)
    out, quotients = pl.pallas_call(
        functools.partial(kernel, S, C, A, nk, nch),
        out_shape=(
            jax.ShapeDtypeStruct((dirs, cols), F32),
            jax.ShapeDtypeStruct((1, dirs), F32),
        ),
        in_specs=[hbm, hbm, vmem, vmem, vmem],
        out_specs=(vmem, vmem),
        scratch_shapes=[
            pltpu.VMEM((rows, cols), BF16),
            pltpu.VMEM((dirs, cols), BF16),
            pltpu.VMEM((A, R, rows), F32),
            pltpu.VMEM((A, R, rows), F32),
            pltpu.VMEM((B, R, rows), F32),
            pltpu.VMEM((G, R, rows), F32),
            pltpu.VMEM((S, dirs, rows), F32),
            pltpu.VMEM((S, 1, rows), jnp.int32),
            pltpu.VMEM((max(S - 1, 1), nch, dirs, ch), F32),
            pltpu.VMEM((S, nch, dirs, ch), F32),
            pltpu.VMEM((S, nch, dirs, ch), F32),
            pltpu.VMEM((N, 1, BLOCK), F32),
            pltpu.VMEM((nch, dirs, ch), F32),
            dma((nk,)), dma, dma((S,)), dma((S,)), dma((A,)), dma((A,)), dma((B,)), dma((B,)),
            dma((G,)), dma((G,)), dma((S, nch)), dma((S, nch)), dma((S,)), dma((S,)), dma, dma,
        ],
        compiler_params=pltpu.CompilerParams(
            collective_id=0, has_side_effects=True, vmem_limit_bytes=67_000_000
        ),
        name="flow_step",
    )(methylation, directions, labels.reshape(1, rows), step_sizes.reshape(1, dirs), supports)
    return out, quotients.reshape(dirs)


def solution(mesh):
    in_specs = (P("samp", "cpg"), P("samp"), P(None, "cpg"), P(), P())
    out_specs = (P(None, "cpg"), P())
    return jax.shard_map(
        functools.partial(per_device, mesh.shape["samp"], mesh.shape["cpg"]),
        mesh=mesh, in_specs=in_specs, out_specs=out_specs, check_vma=False,
    )
```

time: 120 us -> 31.9 us (0.27)
  blocking collectives: 73.1 us -> 0 us
  Pallas kernels: 0 us -> 28.2 us
  waiting for transfers between devices: 19.9 us -> 0 us
  between operations: 14.1 us -> 0.64 us
  matrix products: 6.9 us -> 0 us
  other arithmetic: 5.71 us -> 0 us
  local copies, waits for them, and re-layouts: 0.11 us -> 2.79 us
    psum x3 -> x0, blocking collectives: 73.1 us -> none  [the longest x1 35.5 us: per_device(): projected = lax.psum(partial_proj, 'cpg')]
    pallas_call x0 -> x1, Pallas kernels: none -> 28.2 us  [per_device(): pl.pallas_call(functools.partial(kernel, S, C, A, nk, nch), out_shape=(ja...]
    psum x1 -> x0, waiting for transfers between devices: 19.9 us -> none  [per_device(): gradient = lax.psum(partial_grad, 'samp')]
    dot_general x5 -> x0, matrix products: 6.9 us -> none  [the longest x1 3.37 us: per_device(): lax.dot_general(combined, methylation, (((0,), (0,)), ((), ())), preferre...]
    reduce_sum x6 -> x0, other arithmetic: 2.98 us -> none  [the longest x1 1.17 us: per_device(): sums = lax.psum(jnp.sum(masked * masked, axis=1), 'cpg')]
    unnamed x10 -> x2, local copies, waits for them, and re-layouts: 0.03 us -> 2.79 us
    mul x1 -> x0, other arithmetic: 1.76 us -> none  [per_device(): masked * lax.rsqrt(sums / (KB * BLOCK) + STABILITY_FLOOR)[:, None]]
  transfers between devices with their start and end apart: 1 -> 0, of which waited for: 1 -> 0; matrix products, arithmetic and copies ran while one was open for 0% -> 0% of each run, Pallas kernels for 0% -> 0%
where the time goes in v1:
time: 31.9 us; the launch traced here: 31.7 us
  Pallas kernels  28.2 us (88%)
  local copies, waits for them, and re-layouts  2.79 us (9%)
  between operations  0.64 us (2%)
    pallas_call x1, Pallas kernels, per_device(): pl.pallas_call(functools.partial(kernel, S, C, A, nk, nch), out_shape=(ja...  28.2 us
    unnamed x2, local copies, waits for them, and re-layouts  2.79 us

profile of v1, /device:TPU:0, one launch (start us, length us, event | category | flops | bytes accessed | tf_op | source)
XLA Modules:
  0.0 31.7 jit_solution(1360252962377627743)
XLA Ops:
  0.6 28.2 %flow_step.1 = (f32[8,7168]{1,0:T(8,128)}, f32[1,8]{1,0:T(1,128)}) custom-call(bf16[256,7168]{1,0:T(8,128)(2,1)} %m_hbm.1, bf16[8,7168]{1,0:T(8,128)(2,1)} %d_hbm.1, s32[1,256]{1,0:T(1,128)} %bitcast.3, f32[1,8]{1,0:T(1,128)} %bitcast.4, s32[8,64]{1,0:T(8,128)} %sup_ref.1), custom_call_target="tpu_custom_call" | custom-call | tf_op jit(solution)/shard_map/flow_step/pallas_call | solution.py:247
  28.9 1.6 %copy.9 = f32[8,7168]{1,0:T(8,128)} copy(f32[8,7168]{1,0:T(8,128)} %get-tuple-element.8) | data formatting | bytes 458752
  30.5 1.1 %copy.10 = f32[8]{0:T(128)} copy(f32[8]{0:T(128)} %bitcast.5) | data formatting | bytes 64

commit v2 on v1

--- a/solution.py
+++ b/solution.py
@@ -46,10 +46,10 @@
 def kernel(
     S, C, A, nk, nch,
     m_hbm, d_hbm, lab_ref, step_ref, sup_ref,
-    out_ref, quo_ref,
+    kept_hbm, norm_ref, quo_ref,
     mv, dv, part, abuf, bbuf, pall, proj, lab_all, gsend, grecv, fbuf, sbuf, mask,
     m_sem, d_sem, lab_send, lab_recv, a_send, a_recv, b_send, b_recv, c_send, c_recv,
-    g_send, g_recv, f_send, f_recv, s_send, s_recv,
+    g_send, g_recv, f_send, f_recv, s_send, s_recv, o_sem,
 ):
     B = C // A
     N = S * C
@@ -67,6 +67,13 @@
     me = s * C + c
     mine = s * A + a
 
+    barrier = pltpu.get_barrier_semaphore()
+    partners = [(s, lax.rem(b + r, B) * A + a) for r in range(1, B)]
+    partners += [(lax.rem(s + r, S), c) for r in range(1, S)]
+    partners += [(s, b * A + lax.rem(a + r, A)) for r in range(1, A)]
+    for partner in partners:
+        pl.semaphore_signal(barrier, inc=1, device_id=partner, device_id_type=MESH)
+
     d_copy = pltpu.make_async_copy(d_hbm, dv, d_sem)
     d_copy.start()
     m_copies = []
@@ -75,17 +82,6 @@
         copy = pltpu.make_async_copy(m_hbm.at[:, span], mv.at[:, span], m_sem.at[k])
         copy.start()
         m_copies.append(copy)
-
-    barrier = pltpu.get_barrier_semaphore()
-
-    def greet(r, carry):
-        t = lax.rem(me + r, N)
-        pl.semaphore_signal(
-            barrier, inc=1, device_id=(lax.div(t, C), lax.rem(t, C)), device_id_type=MESH
-        )
-        return carry
-
-    lax.fori_loop(1, N, greet, 0)
 
     lab_all[s] = lab_ref[...]
     sup = sup_ref[...]
@@ -107,7 +103,7 @@
     for i in range(A):
         part[i] = acc[i * R:(i + 1) * R, :]
 
-    pl.semaphore_wait(barrier, N - 1)
+    pl.semaphore_wait(barrier, len(partners))
 
     def remote(src, dst, send, recv, to):
         return pltpu.make_async_remote_copy(
@@ -212,24 +208,41 @@
         ).start()
         return carry
 
-    lax.fori_loop(1, N, tell, 0)
+    if N <= 64:
+        for r in range(1, N):
+            tell(r, 0)
+    else:
+        lax.fori_loop(1, N, tell, 0)
     for r in range(1, S):
         t = lax.rem(s + r, S)
         start(remote(fbuf.at[s], fbuf.at[s], f_send.at[r], f_recv.at[s], (t, c)))
+    out_copies = [pltpu.make_async_copy(fbuf.at[s], kept_hbm.at[s], o_sem.at[0])]
+    out_copies[0].start()
     others = sbuf.at[pl.ds(0, N - 1)]
+    for r in range(1, S):
+        t = lax.rem(s + r, S)
+        remote(fbuf.at[t], fbuf.at[t], f_send.at[r], f_recv.at[t], (s, c)).wait_recv()
+        copy = pltpu.make_async_copy(fbuf.at[t], kept_hbm.at[t], o_sem.at[r])
+        copy.start()
+        out_copies.append(copy)
     pltpu.make_async_copy(others, others, s_recv).wait()
     sums = to_col(jnp.sum(sbuf[...], axis=0), dirs)
     norm = lax.rsqrt(sums / (sup_ref.shape[1] * BLOCK) + STABILITY_FLOOR)
-    for r in range(1, S):
-        t = lax.rem(s + r, S)
-        remote(fbuf.at[t], fbuf.at[t], f_send.at[r], f_recv.at[t], (s, c)).wait_recv()
-    for i in range(S):
-        for k in range(nch):
-            at = i * piece + k * ch
-            out_ref[:, at:at + ch] = fbuf[i, k] * norm
+    norm_ref[...] = jnp.broadcast_to(norm, (dirs, BLOCK))
     for copy in sent:
         copy.wait_send()
     pltpu.make_async_copy(others, others, s_send).wait()
+    for copy in out_copies:
+        copy.wait()
+
+
+def finish(S, nch, ch, kept_ref, norm_ref, quo_in, out_ref, quo_ref):
+    norm = norm_ref[:, :1]
+    for i in range(S):
+        for k in range(nch):
+            at = (i * nch + k) * ch
+            out_ref[:, at:at + ch] = kept_ref[i, k] * norm
+    quo_ref[...] = quo_in[...]
 
 
 def per_device(S, C, methylation, labels, directions, step_sizes, supports):
@@ -244,14 +257,15 @@
     dma = pltpu.SemaphoreType.DMA
     vmem = pl.BlockSpec(memory_space=pltpu.VMEM)
     hbm = pl.BlockSpec(memory_space=pltpu.HBM)
-    out, quotients = pl.pallas_call(
+    kept, norm, quotients = pl.pallas_call(
         functools.partial(kernel, S, C, A, nk, nch),
         out_shape=(
-            jax.ShapeDtypeStruct((dirs, cols), F32),
+            jax.ShapeDtypeStruct((S, nch, dirs, ch), F32),
+            jax.ShapeDtypeStruct((dirs, BLOCK), F32),
             jax.ShapeDtypeStruct((1, dirs), F32),
         ),
         in_specs=[hbm, hbm, vmem, vmem, vmem],
-        out_specs=(vmem, vmem),
+        out_specs=(hbm, vmem, vmem),
         scratch_shapes=[
             pltpu.VMEM((rows, cols), BF16),
             pltpu.VMEM((dirs, cols), BF16),
@@ -268,12 +282,24 @@
             pltpu.VMEM((nch, dirs, ch), F32),
             dma((nk,)), dma, dma((S,)), dma((S,)), dma((A,)), dma((A,)), dma((B,)), dma((B,)),
             dma((G,)), dma((G,)), dma((S, nch)), dma((S, nch)), dma((S,)), dma((S,)), dma, dma,
+            dma((S,)),
         ],
         compiler_params=pltpu.CompilerParams(
             collective_id=0, has_side_effects=True, vmem_limit_bytes=67_000_000
         ),
         name="flow_step",
     )(methylation, directions, labels.reshape(1, rows), step_sizes.reshape(1, dirs), supports)
+    out, quotients = pl.pallas_call(
+        functools.partial(finish, S, nch, ch),
+        out_shape=(
+            jax.ShapeDtypeStruct((dirs, cols), F32),
+            jax.ShapeDtypeStruct((1, dirs), F32),
+        ),
+        in_specs=[vmem, vmem, vmem],
+        out_specs=(vmem, vmem),
+        compiler_params=pltpu.CompilerParams(vmem_limit_bytes=67_000_000),
+        name="finish",
+    )(kept, norm, quotients)
     return out, quotients.reshape(dirs)
 
 

time: 31.9 us -> 30.4 us (0.953)
  local copies, waits for them, and re-layouts: 2.79 us -> 0 us
  Pallas kernels: 28.2 us -> 29.6 us
    unnamed x2 -> x0, local copies, waits for them, and re-layouts: 2.79 us -> none
    pallas_call x0 -> x1, Pallas kernels: none -> 1.72 us  [per_device(): pl.pallas_call(functools.partial(finish, S, nch, ch), out_shape=(jax.Shap...]
    pallas_call x1, Pallas kernels: 28.2 us -> 27.9 us  [per_device(): pl.pallas_call(functools.partial(kernel, S, C, A, nk, nch), out_shape=(ja...]
where the time goes in v2:
time: 30.4 us; the launch traced here: 30.2 us
  Pallas kernels  29.6 us (97%)
  between operations  0.64 us (2%)
    pallas_call x1, Pallas kernels, per_device(): pl.pallas_call(functools.partial(kernel, S, C, A, nk, nch), out_shape=(ja...  27.9 us
    pallas_call x1, Pallas kernels, per_device(): pl.pallas_call(functools.partial(finish, S, nch, ch), out_shape=(jax.Shap...  1.72 us

profile of v2, /device:TPU:0, one launch (start us, length us, event | category | flops | bytes accessed | tf_op | source)
XLA Modules:
  0.0 30.2 jit_solution(6857429165114914804)
XLA Ops:
  0.6 27.9 %flow_step.1 = (f32[2,4,8,896]{3,2,1,0:T(8,128)}, f32[8,128]{1,0:T(8,128)}, f32[1,8]{1,0:T(1,128)}) custom-call(bf16[256,7168]{1,0:T(8,128)(2,1)} %m_hbm.1, bf16[8,7168]{1,0:T(8,128)(2,1)} %d_hbm.1, s32[1,256]{1,0:T(1,128)} %bitcast.3, f32[1,8]{1,0:T(1,128)} %bitcast.4, s32[8,64]{1,0:T(8,128)} %sup_ref.1), custom_call_target="tpu_custom_call" | custom-call | tf_op jit(solution)/shard_map/flow_step/pallas_call | solution.py:260
  28.5 1.7 %finish.1 = (f32[8,7168]{1,0:T(8,128)}, f32[1,8]{1,0:T(1,128)}) custom-call(f32[2,4,8,896]{3,2,1,0:T(8,128)} %get-tuple-element.7.kept_ref, f32[8,128]{1,0:T(8,128)} %get-tuple-element.8.norm_ref, f32[1,8]{1,0:T(1,128)} %get-tuple-element.9.quo_in), custom_call_target="tpu_custom_call" | custom-call | tf_op jit(solution)/shard_map/finish/pallas_call | solution.py:292

commit v3 on v2

--- a/solution.py
+++ b/solution.py
@@ -248,7 +248,7 @@
 def per_device(S, C, methylation, labels, directions, step_sizes, supports):
     rows, cols = methylation.shape
     dirs = directions.shape[0]
-    A = max(d for d in range(1, dirs + 1) if dirs % d == 0 and C % d == 0 and d * d <= C)
+    A = max(d for d in range(1, dirs + 1) if dirs % d == 0 and C % d == 0 and d * d * d <= C)
     B, N, G, R = C // A, S * C, S * A, dirs // A
     piece = cols // S
     nk = divisor(cols // BLOCK, 7)

time: 30.4 us -> 28.9 us (0.951)
  Pallas kernels: 29.6 us -> 28 us
    pallas_call x1, Pallas kernels: 27.9 us -> 26.3 us  [per_device(): pl.pallas_call(functools.partial(kernel, S, C, A, nk, nch), out_shape=(ja...]
where the time goes in v3:
time: 28.9 us; the launch traced here: 28.7 us
  Pallas kernels  28 us (97%)
  between operations  0.64 us (2%)
    pallas_call x1, Pallas kernels, per_device(): pl.pallas_call(functools.partial(kernel, S, C, A, nk, nch), out_shape=(ja...  26.3 us
    pallas_call x1, Pallas kernels, per_device(): pl.pallas_call(functools.partial(finish, S, nch, ch), out_shape=(jax.Shap...  1.72 us

profile of v3, /device:TPU:0, one launch (start us, length us, event | category | flops | bytes accessed | tf_op | source)
XLA Modules:
  0.0 28.7 jit_solution(2466458433510682301)
XLA Ops:
  0.6 26.3 %flow_step.1 = (f32[2,4,8,896]{3,2,1,0:T(8,128)}, f32[8,128]{1,0:T(8,128)}, f32[1,8]{1,0:T(1,128)}) custom-call(bf16[256,7168]{1,0:T(8,128)(2,1)} %m_hbm.1, bf16[8,7168]{1,0:T(8,128)(2,1)} %d_hbm.1, s32[1,256]{1,0:T(1,128)} %bitcast.3, f32[1,8]{1,0:T(1,128)} %bitcast.4, s32[8,64]{1,0:T(8,128)} %sup_ref.1), custom_call_target="tpu_custom_call" | custom-call | tf_op jit(solution)/shard_map/flow_step/pallas_call | solution.py:260
  27.0 1.7 %finish.1 = (f32[8,7168]{1,0:T(8,128)}, f32[1,8]{1,0:T(1,128)}) custom-call(f32[2,4,8,896]{3,2,1,0:T(8,128)} %get-tuple-element.7.kept_ref, f32[8,128]{1,0:T(8,128)} %get-tuple-element.8.norm_ref, f32[1,8]{1,0:T(1,128)} %get-tuple-element.9.quo_in), custom_call_target="tpu_custom_call" | custom-call | tf_op jit(solution)/shard_map/finish/pallas_call | solution.py:292

commit v4 on v3

--- a/solution.py
+++ b/solution.py
@@ -248,7 +248,7 @@
 def per_device(S, C, methylation, labels, directions, step_sizes, supports):
     rows, cols = methylation.shape
     dirs = directions.shape[0]
-    A = max(d for d in range(1, dirs + 1) if dirs % d == 0 and C % d == 0 and d * d * d <= C)
+    A = 1
     B, N, G, R = C // A, S * C, S * A, dirs // A
     piece = cols // S
     nk = divisor(cols // BLOCK, 7)

time: 28.9 us -> 28.5 us (0.986)
  Pallas kernels: 28 us -> 27.7 us
    pallas_call x1, Pallas kernels: 26.3 us -> 25.9 us  [per_device(): pl.pallas_call(functools.partial(kernel, S, C, A, nk, nch), out_shape=(ja...]
where the time goes in v4:
time: 28.5 us; the launch traced here: 28.3 us
  Pallas kernels  27.7 us (97%)
  between operations  0.64 us (2%)
    pallas_call x1, Pallas kernels, per_device(): pl.pallas_call(functools.partial(kernel, S, C, A, nk, nch), out_shape=(ja...  25.9 us
    pallas_call x1, Pallas kernels, per_device(): pl.pallas_call(functools.partial(finish, S, nch, ch), out_shape=(jax.Shap...  1.72 us

profile of v4, /device:TPU:0, one launch (start us, length us, event | category | flops | bytes accessed | tf_op | source)
XLA Modules:
  0.0 28.3 jit_solution(8367610323229534698)
XLA Ops:
  0.6 25.9 %flow_step.1 = (f32[2,4,8,896]{3,2,1,0:T(8,128)}, f32[8,128]{1,0:T(8,128)}, f32[1,8]{1,0:T(1,128)}) custom-call(bf16[256,7168]{1,0:T(8,128)(2,1)} %m_hbm.1, bf16[8,7168]{1,0:T(8,128)(2,1)} %d_hbm.1, s32[1,256]{1,0:T(1,128)} %bitcast.3, f32[1,8]{1,0:T(1,128)} %bitcast.4, s32[8,64]{1,0:T(8,128)} %sup_ref.1), custom_call_target="tpu_custom_call" | custom-call | tf_op jit(solution)/shard_map/flow_step/pallas_call | solution.py:260
  26.6 1.7 %finish.1 = (f32[8,7168]{1,0:T(8,128)}, f32[1,8]{1,0:T(1,128)}) custom-call(f32[2,4,8,896]{3,2,1,0:T(8,128)} %get-tuple-element.7.kept_ref, f32[8,128]{1,0:T(8,128)} %get-tuple-element.8.norm_ref, f32[1,8]{1,0:T(1,128)} %get-tuple-element.9.quo_in), custom_call_target="tpu_custom_call" | custom-call | tf_op jit(solution)/shard_map/finish/pallas_call | solution.py:292
